TPU v7x, 32 devices: a whole 2x2x4 slice. The times are simulated.
32 devices in a mesh: grid: 8 (over z, y), snap: 4 (over x, core).
Axes of the slice: x: 2, y: 2, z: 4, core: 2. Of those that a mesh axis runs over, the one named last changes fastest.
Arguments:
- fields: bfloat16 [49152, 1024], P('grid', 'snap'), may hold values from -40 to 40
- start_local: float32 [1024, 128], P('snap'), may hold values from -6 to 6
- start_pair: float32 [2, 256, 128], replicated, may hold values from -6 to 6
- start_root: float32 [256, 128], replicated, may hold values from -6 to 6
Outputs:
- modes: bfloat16 [49152, 128], P(('grid', 'snap'))
All inputs are finite; a program needn't handle non-finite values.
Results may differ from a plain program's by a relative error of at most 0.0055.
Values may be sent and summed in bfloat16 or wider, within the bound.
No kernel may reach another device: no remote copies, remote signals or barrier semaphores. Data moves between devices by JAX's collectives and lax.ppermute only.
A program may use at most 64 MiB of HBM per device.

v0:
```python
import jax
import jax.numpy as jnp
from jax import lax
from jax.sharding import PartitionSpec as P

POWER = 2
NEWTON = 8


def from_partner(value, axis, bit):
    mask = 2**bit
    pairs = [(source, source ^ mask) for source in range(lax.axis_size(axis))]
    return lax.ppermute(value, axis, pairs)


def polar_basis(gram_matrix, initial):
    current = initial
    for power_step in range(POWER):
        product = jnp.dot(gram_matrix, current, precision=lax.Precision.HIGHEST)
        iterate = product / jnp.sqrt(jnp.sum(product * product) + 1e-06)
        for newton_step in range(NEWTON):
            inner_gram = jnp.dot(iterate.T, iterate, precision=lax.Precision.HIGHEST)
            iterate = 1.5 * iterate - 0.5 * jnp.dot(
                iterate, inner_gram, precision=lax.Precision.HIGHEST
            )
        current = iterate
    return current


def rotate(joined, rotation):
    return jnp.dot(
        joined, rotation.astype(jnp.bfloat16), preferred_element_type=jnp.float32
    ).astype(jnp.bfloat16)


def on_device(fields, start_local, start_pair, start_root):
    local_rows = fields.shape[0]
    inverse_count = 1.0 / (local_rows * lax.axis_size("grid"))
    partial_gram = jnp.dot(fields.T, fields, preferred_element_type=jnp.float32)
    gram_sum = lax.psum(partial_gram, "grid") * inverse_count
    rotation = polar_basis(gram_sum, start_local)
    leaf_field = rotate(fields, rotation)
    position = lax.axis_index("snap")
    low_bit = position % 2
    high_bit = position // 2
    node_start = lax.dynamic_index_in_dim(start_pair, high_bit, 0, keepdims=False)
    quarter = local_rows // 4
    partner = from_partner(leaf_field, "snap", 0)
    lower_part = jnp.where(low_bit == 0, leaf_field, partner)
    upper_part = jnp.where(low_bit == 0, partner, leaf_field)
    joined = jnp.concatenate([lower_part, upper_part], axis=1)
    partial_gram = jnp.dot(joined.T, joined, preferred_element_type=jnp.float32)
    gram_sum = lax.psum(partial_gram, "grid") * inverse_count
    branch = rotate(joined, polar_basis(gram_sum, node_start))
    partner = from_partner(branch, "snap", 1)
    lower_part = jnp.where(high_bit == 0, branch, partner)
    upper_part = jnp.where(high_bit == 0, partner, branch)
    joined = jnp.concatenate([lower_part, upper_part], axis=1)
    partial_gram = jnp.dot(joined.T, joined, preferred_element_type=jnp.float32)
    gram_sum = lax.psum(partial_gram, "grid") * inverse_count
    rotation = polar_basis(gram_sum, start_root)
    own_rows = lax.dynamic_slice_in_dim(joined, position * quarter, quarter, 0)
    return rotate(own_rows, rotation)


def solution(mesh):
    in_specs = (P("grid", "snap"), P("snap", None), P(), P())
    out_specs = P(("grid", "snap"), None)
    return jax.shard_map(
        on_device, mesh=mesh, in_specs=in_specs, out_specs=out_specs, check_vma=False
    )
```

profile of v0, /device:TPU:0, one launch (start us, length us, event | category | flops | bytes accessed | tf_op | source)
XLA Modules:
  0.0 331.3 jit_solution(1341703258600756548)
XLA Ops:
  6.5 1.9 copy-done
  8.4 1.7 fusion.94
  10.2 74.2 %all-reduce.4.cloned.1.call-done = f32[256,256]{1,0:T(8,128)} async-done(((f32[256,256]{1,0:T(8,128)}), f32[256,256]{1,0:T(8,128)}) %all-reduce.4.cloned.1.call-update) | async-done | bytes 262160 | tf_op jit(solution)/shard_map/psum | solution.py:40
  84.4 1.9 multiply_reduce_fusion.5
  87.1 0.4 fusion.76
  88.4 0.4 fusion.96
  92.4 1.0 multiply_reduce_fusion.4
  94.0 0.4 fusion.77
  99.3 2.3 fusion
  101.7 3.7 %collective-permute-done = bf16[6144,128]{0,1:T(8,128)(2,1)} collective-permute-done((bf16[6144,128]{0,1:T(8,128)(2,1)}, bf16[6144,128]{0,1:T(8,128)(2,1)}, u32[]{:S(2)}, u32[]{:S(2)}) %collective-permute-start) | collective-permute-done | bytes 1572896 | tf_op jit(solution)/shard_map/ppermute | solution.py:13
  105.4 2.1 broadcast_select_fusion.1
  107.5 1.1 copy-done.5
  108.7 0.5 copy-done.7
  109.2 1.7 fusion.2
  111.1 70.1 %all-reduce.6.cloned.1.call-done = f32[256,256]{1,0:T(8,128)} async-done(((f32[256,256]{1,0:T(8,128)}), f32[256,256]{1,0:T(8,128)}) %all-reduce.6.cloned.1.call-update) | async-done | bytes 262160 | tf_op jit(solution)/shard_map/psum | solution.py:53
  181.3 1.9 multiply_reduce_fusion.3
  183.9 0.4 fusion.78
  189.2 1.0 multiply_reduce_fusion.2
  190.9 0.4 fusion.79
  196.2 1.8 convolution_convert_fusion
  198.0 1.5 collective-permute-start.1
  199.4 33.1 %collective-permute-done.1 = bf16[6144,128]{0,1:T(8,128)(2,1)} collective-permute-done((bf16[6144,128]{0,1:T(8,128)(2,1)}, bf16[6144,128]{0,1:T(8,128)(2,1)}, u32[]{:S(2)}, u32[]{:S(2)}) %collective-permute-start.1) | collective-permute-done | bytes 1572896 | tf_op jit(solution)/shard_map/ppermute | solution.py:13
  232.6 2.1 broadcast_select_fusion.3
  234.7 1.1 copy-done.1
  235.8 0.5 copy-done.3
  236.3 1.7 fusion.1
  238.1 70.4 %all-reduce.8.cloned.1.call-done = f32[256,256]{1,0:T(8,128)} async-done(((f32[256,256]{1,0:T(8,128)}), f32[256,256]{1,0:T(8,128)}) %all-reduce.8.cloned.1.call-update) | async-done | bytes 262160 | tf_op jit(solution)/shard_map/psum | solution.py:60
  308.4 1.9 multiply_reduce_fusion.1
  311.1 0.6 fusion.80
  316.6 1.0 multiply_reduce_fusion
  318.3 0.4 fusion.81
  323.6 1.2 convolution_convert_fusion.2
  (121 shorter events, 28.8 us)
Async XLA Ops:
  6.5 1.9 copy-start
  6.5 77.9 %copy-start.12 = (f32[256,128]{1,0:T(8,128)S(1)}, f32[256,128]{1,0:T(8,128)}, u32[]{:S(2)}) copy-start(f32[256,128]{1,0:T(8,128)} %param.5) | copy-start | bytes 393220
  6.5 77.9 %all-reduce.4.cloned.1.call-start = ((), (), s32[]{:S(2)}) async-start(), calls=%async_computation | async-start | bytes 524288 | tf_op jit(solution)/shard_map/psum | solution.py:40
  10.2 171.1 %all-reduce.6.cloned.1.call-start = ((), (), s32[]{:S(2)}) async-start(), calls=%async_computation.1 | async-start | bytes 524288 | tf_op jit(solution)/shard_map/psum | solution.py:53
  89.1 3.3 %copy-start.10 = (f32[256,256]{1,0:T(8,128)S(1)}, f32[256,256]{1,0:T(8,128)}, u32[]{:S(2)}) copy-start(f32[256,256]{1,0:T(8,128)} %all-reduce.4.cloned.1.call-done) | copy-start | bytes 786436
  101.7 3.8 %collective-permute-start = (bf16[6144,128]{0,1:T(8,128)(2,1)}, bf16[6144,128]{0,1:T(8,128)(2,1)}, u32[]{:S(2)}, u32[]{:S(2)}) collective-permute-start(bf16[6144,128]{0,1:T(8,128)(2,1)} %fusion), channel_id=1, source_target_pairs={{0,1},{1,0},{2,3},{3,2},{4,5},{5,4},{6,7},{7,6},{8,9},{9,8},{10,11... | collective-permute-start | bytes 4718600 | tf_op jit(solution)/shard_map/ppermute | solution.py:13
  107.5 1.2 copy-start.5
  107.5 1.6 copy-start.7
  109.1 72.1 %copy-start.14 = (f32[2,256,128]{2,1,0:T(8,128)S(1)}, f32[2,256,128]{2,1,0:T(8,128)}, u32[]{:S(2)}) copy-start(f32[2,256,128]{2,1,0:T(8,128)} %param.6) | copy-start | bytes 786436
  110.9 197.5 %all-reduce.8.cloned.1.call-start = ((), (), s32[]{:S(2)}) async-start(), calls=%async_computation.2 | async-start | bytes 524288 | tf_op jit(solution)/shard_map/psum | solution.py:60
  185.9 3.3 %copy-start.11 = (f32[256,256]{1,0:T(8,128)S(1)}, f32[256,256]{1,0:T(8,128)}, u32[]{:S(2)}) copy-start(f32[256,256]{1,0:T(8,128)} %all-reduce.6.cloned.1.call-done) | copy-start | bytes 786436
  192.9 3.3 %copy-start.6 = (bf16[6144,128]{0,1:T(8,128)(2,1)S(1)}, bf16[6144,128]{0,1:T(8,128)(2,1)}, u32[]{:S(2)}) copy-start(bf16[6144,128]{0,1:T(8,128)(2,1)} %copy-done.5) | copy-start | bytes 4718596
  192.9 3.3 %copy-start.8 = (bf16[6144,128]{0,1:T(8,128)(2,1)S(1)}, bf16[6144,128]{0,1:T(8,128)(2,1)}, u32[]{:S(2)}) copy-start(bf16[6144,128]{0,1:T(8,128)(2,1)} %copy-done.7) | copy-start | bytes 4718596
  198.0 34.6 %collective-permute-start.1 = (bf16[6144,128]{0,1:T(8,128)(2,1)}, bf16[6144,128]{0,1:T(8,128)(2,1)}, u32[]{:S(2)}, u32[]{:S(2)}) collective-permute-start(bf16[6144,128]{0,1:T(8,128)(2,1)} %convolution_convert_fusion), channel_id=1, source_target_pairs={{0,2},{1,3},{2,0},{3,1},{4,6},{5,7},{6,4},{7,5},{8,10},{9,11},{10,... | collective-permute-start | bytes 4718600 | tf_op jit(solution)/shard_map/ppermute | solution.py:13
  234.7 1.1 copy-start.1
  234.7 1.6 copy-start.3
  236.3 72.1 %copy-start.13 = (f32[256,128]{1,0:T(8,128)S(1)}, f32[256,128]{1,0:T(8,128)}, u32[]{:S(2)}) copy-start(f32[256,128]{1,0:T(8,128)} %param.7) | copy-start | bytes 393220
  313.3 3.3 %copy-start.9 = (f32[256,256]{1,0:T(8,128)S(1)}, f32[256,256]{1,0:T(8,128)}, u32[]{:S(2)}) copy-start(f32[256,256]{1,0:T(8,128)} %all-reduce.8.cloned.1.call-done) | copy-start | bytes 786436
  320.2 3.3 %copy-start.2 = (bf16[6144,128]{0,1:T(8,128)(2,1)S(1)}, bf16[6144,128]{0,1:T(8,128)(2,1)}, u32[]{:S(2)}) copy-start(bf16[6144,128]{0,1:T(8,128)(2,1)} %copy-done.1) | copy-start | bytes 4718596
  320.3 3.3 %copy-start.4 = (bf16[6144,128]{0,1:T(8,128)(2,1)S(1)}, bf16[6144,128]{0,1:T(8,128)(2,1)}, u32[]{:S(2)}) copy-start(bf16[6144,128]{0,1:T(8,128)(2,1)} %copy-done.3) | copy-start | bytes 4718596
Sparse Core Ops, SparseCore 0:
  10.7 73.7 all-reduce.3
  111.0 70.1 all-reduce.5
  238.2 70.1 all-reduce.7
where the time goes:
time: 332 us; the launch traced here: 331 us
  waiting for transfers between devices  252 us (76%)
  matrix products  50.5 us (15%)
  between operations  18 us (5%)
  local copies, waits for them, and re-layouts  5.19 us (2%)
  other arithmetic  4.18 us (1%)
    psum x3, waiting for transfers between devices, on_device(): gram_sum = lax.psum(partial_gram, 'grid') * inverse_count  215 us
    ppermute x2, waiting for transfers between devices, from_partner(): return lax.ppermute(value, axis, pairs)  36.9 us
    dot_general x48, matrix products, polar_basis(): inner_gram = jnp.dot(iterate.T, iterate, precision=lax.Precision.HIGHEST)  18.8 us
    dot_general x48, matrix products, polar_basis(): jnp.dot(iterate, inner_gram, precision=lax.Precision.HIGHEST)  12.6 us
    dot_general x6, matrix products, polar_basis(): product = jnp.dot(gram_matrix, current, precision=lax.Precision.HIGHEST)  8.74 us
  transfers between devices with their start and end apart: 5, of which 5 were waited for; matrix products, arithmetic and copies ran while one was open for 0% of the time, Pallas kernels for 0%

commit v1 on v0

--- a/solution.py
+++ b/solution.py
@@ -37,7 +37,7 @@
     local_rows = fields.shape[0]
     inverse_count = 1.0 / (local_rows * lax.axis_size("grid"))
     partial_gram = jnp.dot(fields.T, fields, preferred_element_type=jnp.float32)
-    gram_sum = lax.psum(partial_gram, "grid") * inverse_count
+    gram_sum = jnp.sum(lax.all_gather(partial_gram, "grid"), axis=0) * inverse_count
     rotation = polar_basis(gram_sum, start_local)
     leaf_field = rotate(fields, rotation)
     position = lax.axis_index("snap")

time: 332 us -> 312 us (0.940)
  waiting for transfers between devices: 252 us -> 229 us
    psum x3 -> x2, waiting for transfers between devices: 215 us -> 140 us  [on_device(): gram_sum = lax.psum(partial_gram, 'grid') * inverse_count]
    all_gather x0 -> x1, waiting for transfers between devices: none -> 51.9 us  [on_device(): lax.all_gather(partial_gram, 'grid')]
where the time goes in v1:
time: 312 us
  waiting for transfers between devices  229 us (73%)
  matrix products  52.3 us (17%)
  between operations  18.1 us (6%)
  other arithmetic  5.93 us (2%)
  local copies, waits for them, and re-layouts  5.19 us (2%)
    psum x2, waiting for transfers between devices, on_device(): gram_sum = lax.psum(partial_gram, 'grid') * inverse_count  140 us
    all_gather x1, waiting for transfers between devices, on_device(): lax.all_gather(partial_gram, 'grid')  51.9 us
    ppermute x2, waiting for transfers between devices, from_partner(): return lax.ppermute(value, axis, pairs)  36.9 us
    dot_general x48, matrix products, polar_basis(): inner_gram = jnp.dot(iterate.T, iterate, precision=lax.Precision.HIGHEST)  19.8 us
    dot_general x48, matrix products, polar_basis(): jnp.dot(iterate, inner_gram, precision=lax.Precision.HIGHEST)  13.6 us
    dot_general x6, matrix products, polar_basis(): product = jnp.dot(gram_matrix, current, precision=lax.Precision.HIGHEST)  8.52 us
  transfers between devices with their start and end apart: 5, of which 5 were waited for; matrix products, arithmetic and copies ran while one was open for 0% of the time, Pallas kernels for 0%

profile of v1, /device:TPU:0, one launch (start us, length us, event | category | flops | bytes accessed | tf_op | source)
XLA Modules:
  0.0 311.8 jit_solution(10444998393201040242)
XLA Ops:
  6.5 1.9 copy-done
  8.4 1.7 fusion.94
  10.2 51.9 %all-gather.3.cloned.1.call-done = f32[2048,256]{1,0:T(8,128)} async-done(((f32[256,256]{1,0:T(8,128)}), f32[2048,256]{1,0:T(8,128)}) %all-gather.3.cloned.1.call-update) | async-done | bytes 2097168 | tf_op jit(solution)/shard_map/all_gather | solution.py:40
  62.1 1.8 reduce_sum.63
  63.9 1.7 multiply_reduce_fusion.5
  66.3 1.4 fusion.76
  67.7 1.2 fusion.3
  73.6 1.0 multiply_reduce_fusion.4
  75.3 0.4 fusion.77
  80.6 2.3 fusion
  82.9 3.7 %collective-permute-done = bf16[6144,128]{0,1:T(8,128)(2,1)} collective-permute-done((bf16[6144,128]{0,1:T(8,128)(2,1)}, bf16[6144,128]{0,1:T(8,128)(2,1)}, u32[]{:S(2)}, u32[]{:S(2)}) %collective-permute-start) | collective-permute-done | bytes 1572896 | tf_op jit(solution)/shard_map/ppermute | solution.py:13
  86.6 2.1 broadcast_select_fusion.1
  88.8 1.1 copy-done.5
  89.9 0.5 copy-done.7
  90.4 1.7 fusion.2
  92.4 69.4 %all-reduce.3.cloned.1.call-done = f32[256,256]{1,0:T(8,128)} async-done(((f32[256,256]{1,0:T(8,128)}), f32[256,256]{1,0:T(8,128)}) %all-reduce.3.cloned.1.call-update) | async-done | bytes 262160 | tf_op jit(solution)/shard_map/psum | solution.py:53
  161.8 1.9 multiply_reduce_fusion.3
  164.4 0.4 fusion.78
  169.8 1.0 multiply_reduce_fusion.2
  171.4 0.4 fusion.79
  176.8 1.8 convolution_convert_fusion
  178.5 1.5 collective-permute-start.1
  180.0 33.1 %collective-permute-done.1 = bf16[6144,128]{0,1:T(8,128)(2,1)} collective-permute-done((bf16[6144,128]{0,1:T(8,128)(2,1)}, bf16[6144,128]{0,1:T(8,128)(2,1)}, u32[]{:S(2)}, u32[]{:S(2)}) %collective-permute-start.1) | collective-permute-done | bytes 1572896 | tf_op jit(solution)/shard_map/ppermute | solution.py:13
  213.1 2.1 broadcast_select_fusion.3
  215.3 1.1 copy-done.1
  216.4 0.5 copy-done.3
  216.9 1.7 fusion.1
  218.6 70.3 %all-reduce.5.cloned.1.call-done = f32[256,256]{1,0:T(8,128)} async-done(((f32[256,256]{1,0:T(8,128)}), f32[256,256]{1,0:T(8,128)}) %all-reduce.5.cloned.1.call-update) | async-done | bytes 262160 | tf_op jit(solution)/shard_map/psum | solution.py:60
  289.0 1.9 multiply_reduce_fusion.1
  291.6 0.6 fusion.80
  297.1 1.0 multiply_reduce_fusion
  304.1 1.2 convolution_convert_fusion.2
  (120 shorter events, 29.3 us)
Async XLA Ops:
  6.5 1.9 copy-start
  6.5 55.6 %all-gather.3.cloned.1.call-start = ((), (), s32[]{:S(2)}) async-start(), calls=%async_computation.2 | async-start | bytes 2359296 | tf_op jit(solution)/shard_map/all_gather | solution.py:40
  10.1 53.8 %copy-start.11 = (f32[256,128]{1,0:T(8,128)S(1)}, f32[256,128]{1,0:T(8,128)}, u32[]{:S(2)}) copy-start(f32[256,128]{1,0:T(8,128)} %param.5) | copy-start | bytes 393220
  10.2 151.6 %all-reduce.3.cloned.1.call-start = ((), (), s32[]{:S(2)}) async-start(), calls=%async_computation | async-start | bytes 524288 | tf_op jit(solution)/shard_map/psum | solution.py:53
  82.9 3.8 %collective-permute-start = (bf16[6144,128]{0,1:T(8,128)(2,1)}, bf16[6144,128]{0,1:T(8,128)(2,1)}, u32[]{:S(2)}, u32[]{:S(2)}) collective-permute-start(bf16[6144,128]{0,1:T(8,128)(2,1)} %fusion), channel_id=1, source_target_pairs={{0,1},{1,0},{2,3},{3,2},{4,5},{5,4},{6,7},{7,6},{8,9},{9,8},{10,11... | collective-permute-start | bytes 4718600 | tf_op jit(solution)/shard_map/ppermute | solution.py:13
  88.7 1.2 copy-start.5
  88.7 1.6 copy-start.7
  90.4 71.4 %copy-start.13 = (f32[2,256,128]{2,1,0:T(8,128)S(1)}, f32[2,256,128]{2,1,0:T(8,128)}, u32[]{:S(2)}) copy-start(f32[2,256,128]{2,1,0:T(8,128)} %param.6) | copy-start | bytes 786436
  92.1 196.8 %all-reduce.5.cloned.1.call-start = ((), (), s32[]{:S(2)}) async-start(), calls=%async_computation.1 | async-start | bytes 524288 | tf_op jit(solution)/shard_map/psum | solution.py:60
  166.4 3.3 %copy-start.10 = (f32[256,256]{1,0:T(8,128)S(1)}, f32[256,256]{1,0:T(8,128)}, u32[]{:S(2)}) copy-start(f32[256,256]{1,0:T(8,128)} %all-reduce.3.cloned.1.call-done) | copy-start | bytes 786436
  173.4 3.3 %copy-start.6 = (bf16[6144,128]{0,1:T(8,128)(2,1)S(1)}, bf16[6144,128]{0,1:T(8,128)(2,1)}, u32[]{:S(2)}) copy-start(bf16[6144,128]{0,1:T(8,128)(2,1)} %copy-done.5) | copy-start | bytes 4718596
  173.4 3.3 %copy-start.8 = (bf16[6144,128]{0,1:T(8,128)(2,1)S(1)}, bf16[6144,128]{0,1:T(8,128)(2,1)}, u32[]{:S(2)}) copy-start(bf16[6144,128]{0,1:T(8,128)(2,1)} %copy-done.7) | copy-start | bytes 4718596
  178.5 34.6 %collective-permute-start.1 = (bf16[6144,128]{0,1:T(8,128)(2,1)}, bf16[6144,128]{0,1:T(8,128)(2,1)}, u32[]{:S(2)}, u32[]{:S(2)}) collective-permute-start(bf16[6144,128]{0,1:T(8,128)(2,1)} %convolution_convert_fusion), channel_id=1, source_target_pairs={{0,2},{1,3},{2,0},{3,1},{4,6},{5,7},{6,4},{7,5},{8,10},{9,11},{10,... | collective-permute-start | bytes 4718600 | tf_op jit(solution)/shard_map/ppermute | solution.py:13
  215.2 1.2 copy-start.1
  215.2 1.6 copy-start.3
  216.9 72.1 %copy-start.12 = (f32[256,128]{1,0:T(8,128)S(1)}, f32[256,128]{1,0:T(8,128)}, u32[]{:S(2)}) copy-start(f32[256,128]{1,0:T(8,128)} %param.7) | copy-start | bytes 393220
  293.8 3.3 %copy-start.9 = (f32[256,256]{1,0:T(8,128)S(1)}, f32[256,256]{1,0:T(8,128)}, u32[]{:S(2)}) copy-start(f32[256,256]{1,0:T(8,128)} %all-reduce.5.cloned.1.call-done) | copy-start | bytes 786436
  300.8 3.3 %copy-start.2 = (bf16[6144,128]{0,1:T(8,128)(2,1)S(1)}, bf16[6144,128]{0,1:T(8,128)(2,1)}, u32[]{:S(2)}) copy-start(bf16[6144,128]{0,1:T(8,128)(2,1)} %copy-done.1) | copy-start | bytes 4718596
  300.8 3.3 %copy-start.4 = (bf16[6144,128]{0,1:T(8,128)(2,1)S(1)}, bf16[6144,128]{0,1:T(8,128)(2,1)}, u32[]{:S(2)}) copy-start(bf16[6144,128]{0,1:T(8,128)(2,1)} %copy-done.3) | copy-start | bytes 4718596
Sparse Core Ops, SparseCore 0:
  10.3 51.7 all-gather.2
  92.3 69.5 all-reduce.2
  218.7 70.1 all-reduce.4
